TPU v7x, 128 devices: a whole 4x4x4 slice. The times are simulated.
128 devices in a mesh: section: 16 (over z_hi, y, core), seq: 8 (over x, z_lo).
Axes of the slice: x: 4, y: 4, z: 4 (z_hi: 2, z_lo: 2; z = z_hi * 2 + z_lo), core: 2. Of those that a mesh axis runs over, the one named last changes fastest.
Arguments:
- forward_rows: bfloat16 [16, 1024, 4096], P('section', 'seq'), may hold values from -54 to 54
- saved_rows: bfloat16 [16, 1024, 4096], P('section', 'seq'), may hold values from -54 to 54
- output_grad: bfloat16 [16, 1024, 4096], P('section', 'seq'), may hold values from -6 to 6
- forward_docs: int32 [16, 1024], replicated, may hold values from 0 to 3, never falling along the last dimension, each value on 1 to 512 neighbouring positions
- backward_docs: int32 [16, 1024], replicated, may hold values from 0 to 3, never falling along the last dimension, each value on 1 to 512 neighbouring positions
- norm_gain: float32 [16, 4096], P('section'), may hold values from 0.7 to 8
- query_weight: bfloat16 [16, 4096, 4096], P('section', None, 'seq'), may hold values from -0.09375 to 0.09375
- key_matrix: bfloat16 [16, 4096, 1024], P('section', None, 'seq'), may hold values from -0.09375 to 0.09375
- value_matrix: bfloat16 [16, 4096, 1024], P('section', None, 'seq'), may hold values from -0.09375 to 0.09375
Outputs:
- section_output: bfloat16 [16, 1024, 4096], P('section', 'seq')
- input_grad: bfloat16 [16, 1024, 4096], P('section', 'seq')
Inputs may be any that keep to these rules, and one draw needn't show every extreme that they name: `forward_docs`: document ids never fall along a row; every document holds at most 512 tokens and some document of each row holds exactly that many. `backward_docs`: document ids never fall along a row; every document holds at most 512 tokens and some document of each row holds exactly that many.
All inputs are finite; a program needn't handle non-finite values.
Results may differ from a plain program's by a relative error of at most 0.017.
The roundings to bfloat16 on the way count: a program that leaves them out, or rounds other values in their place, can miss the bound.
Values may be sent and summed in bfloat16 or wider, within the bound.
A program may use at most 192 MiB of HBM per device.

v0:
```python
import jax
import jax.numpy as jnp
from jax import lax
from jax.sharding import PartitionSpec as P

MODEL_WIDTH = 4096
HEAD_SIZE = 128
epsilon = 1e-05
rope_base = 500000.0


def passed_along(shard, axis, by):
    peers = lax.axis_size(axis)
    pairs = [(i, i + by) for i in range(peers) if 0 <= i + by < peers]
    return lax.ppermute(shard, axis, pairs)


def rotation_tables(positions):
    half = HEAD_SIZE // 2
    freqs = rope_base ** (-(jnp.arange(half, dtype=jnp.float32) * 2.0 / HEAD_SIZE))
    angles = positions[:, None] * freqs[None, :]
    return (jnp.cos(angles), jnp.sin(angles))


def rotate(values, cosines, sines, sign):
    half = values.shape[-1] // 2
    extra = (1,) * (values.ndim - 2)
    cos_wide = cosines.reshape(cosines.shape[:1] + extra + cosines.shape[1:])
    sin_wide = sines.reshape(sines.shape[:1] + extra + sines.shape[1:])
    first = values[..., :half]
    second = values[..., half:]
    return jnp.concatenate(
        [first * cos_wide - sign * second * sin_wide, second * cos_wide + sign * first * sin_wide],
        axis=-1,
    )


def pair_mask(row_docs, col_docs, row_begin):
    row_pos = row_begin + lax.iota(jnp.int32, row_docs.shape[0])
    col_pos = lax.iota(jnp.int32, col_docs.shape[0])
    return (col_pos[None, :] <= row_pos[:, None]) & (row_docs[:, None] == col_docs[None, :])


def block_probs(query_block, key_heads, allowed):
    scores = jnp.einsum(
        "tjgd,sjd->jgts", query_block, key_heads, preferred_element_type=jnp.float32
    ) * HEAD_SIZE ** (-0.5)
    scores = jnp.where(allowed, scores, -1e30)
    row_top = jnp.max(scores, axis=-1, keepdims=True)
    exp_scores = jnp.where(allowed, jnp.exp(scores - row_top), 0.0)
    return exp_scores / jnp.sum(exp_scores, axis=-1, keepdims=True)


def attend(query_rows_local, key_rows, value_rows, documents):
    sequence_length = query_rows_local.shape[0]
    groups = key_rows.shape[1] // HEAD_SIZE
    group_size = query_rows_local.shape[1] // key_rows.shape[1]
    query_head_count = query_rows_local.reshape(sequence_length, groups, group_size, HEAD_SIZE)
    key_heads = key_rows.reshape(sequence_length, groups, HEAD_SIZE)
    value_heads = value_rows.reshape(sequence_length, groups, HEAD_SIZE)
    block_rows = min(512, sequence_length)
    pieces = []
    for block_index in range(sequence_length // block_rows):
        begin_row = block_index * block_rows
        end_row = begin_row + block_rows
        allowed = pair_mask(documents[begin_row:end_row], documents[:end_row], begin_row)
        probability = block_probs(
            query_head_count[begin_row:end_row], key_heads[:end_row], allowed
        ).astype(jnp.bfloat16)
        mixed_rows = jnp.einsum(
            "jgts,sjd->tjgd", probability, value_heads[:end_row], preferred_element_type=jnp.float32
        )
        pieces.append(mixed_rows.astype(jnp.bfloat16))
    return lax.optimization_barrier(
        jnp.concatenate(pieces, 0).reshape(sequence_length, query_rows_local.shape[1])
    )


def attend_back(query_rows_local, key_rows, value_rows, output_gradient, documents, cosines, sines):
    sequence_length = query_rows_local.shape[0]
    groups = key_rows.shape[1] // HEAD_SIZE
    group_size = query_rows_local.shape[1] // key_rows.shape[1]
    query_head_count = query_rows_local.reshape(sequence_length, groups, group_size, HEAD_SIZE)
    key_heads = key_rows.reshape(sequence_length, groups, HEAD_SIZE)
    value_heads = value_rows.reshape(sequence_length, groups, HEAD_SIZE)
    head_gradients = output_gradient.reshape(sequence_length, groups, group_size, HEAD_SIZE)
    scale = HEAD_SIZE ** (-0.5)
    key_grad = jnp.zeros((sequence_length, groups, HEAD_SIZE), jnp.float32)
    value_grad = jnp.zeros((sequence_length, groups, HEAD_SIZE), jnp.float32)
    block_rows = min(512, sequence_length)
    query_pieces = []
    for block_index in range(sequence_length // block_rows):
        begin_row = block_index * block_rows
        end_row = begin_row + block_rows
        allowed = pair_mask(documents[begin_row:end_row], documents[:end_row], begin_row)
        query_block = query_head_count[begin_row:end_row]
        grad_block = head_gradients[begin_row:end_row]
        probability = block_probs(query_block, key_heads[:end_row], allowed)
        grad_probs = jnp.einsum(
            "tjgd,sjd->jgts", grad_block, value_heads[:end_row], preferred_element_type=jnp.float32
        )
        row_delta = jnp.sum(probability * grad_probs, axis=-1, keepdims=True)
        grad_scores = (probability * (grad_probs - row_delta)).astype(jnp.bfloat16)
        query_piece = (
            jnp.einsum(
                "jgts,sjd->tjgd",
                grad_scores,
                key_heads[:end_row],
                preferred_element_type=jnp.float32,
            )
            * scale
        )
        query_piece = rotate(
            query_piece, cosines[begin_row:end_row], sines[begin_row:end_row], -1.0
        )
        query_pieces.append(query_piece.astype(jnp.bfloat16))
        key_grad = key_grad.at[:end_row].add(
            jnp.einsum(
                "jgts,tjgd->sjd", grad_scores, query_block, preferred_element_type=jnp.float32
            )
            * scale
        )
        value_grad = value_grad.at[:end_row].add(
            jnp.einsum(
                "jgts,tjgd->sjd",
                probability.astype(jnp.bfloat16),
                grad_block,
                preferred_element_type=jnp.float32,
            )
        )
    query_grad = jnp.concatenate(query_pieces, 0).reshape(
        sequence_length, query_rows_local.shape[1]
    )
    key_grad = (
        rotate(key_grad, cosines, sines, -1.0)
        .astype(jnp.bfloat16)
        .reshape(sequence_length, groups * HEAD_SIZE)
    )
    value_grad = value_grad.astype(jnp.bfloat16).reshape(sequence_length, groups * HEAD_SIZE)
    return lax.optimization_barrier((query_grad, key_grad, value_grad))


def token_scale(hidden):
    return lax.rsqrt(jnp.mean(hidden * hidden, axis=-1, keepdims=True) + epsilon)


def heads_inputs(rows_whole, weights):
    query_weight, key_matrix, value_matrix = weights
    sequence_length = rows_whole.shape[0]
    cosines, sines = rotation_tables(jnp.arange(sequence_length, dtype=jnp.float32))
    query_proj = jnp.dot(rows_whole, query_weight, preferred_element_type=jnp.float32)
    key_projected_rows = jnp.dot(rows_whole, key_matrix, preferred_element_type=jnp.float32)
    value_projected_rows = jnp.dot(rows_whole, value_matrix, preferred_element_type=jnp.float32)
    query_rows_local = (
        rotate(query_proj.reshape(sequence_length, -1, HEAD_SIZE), cosines, sines, 1.0)
        .reshape(sequence_length, -1)
        .astype(jnp.bfloat16)
    )
    key_rows = (
        rotate(key_projected_rows.reshape(sequence_length, -1, HEAD_SIZE), cosines, sines, 1.0)
        .reshape(sequence_length, -1)
        .astype(jnp.bfloat16)
    )
    value_rows = value_projected_rows.astype(jnp.bfloat16)
    return (query_rows_local, key_rows, value_rows, cosines, sines)


def body(
    forward_rows,
    saved_rows,
    output_grad,
    forward_docs,
    backward_docs,
    norm_gain,
    query_weight,
    key_matrix,
    value_matrix,
):
    section_index = lax.axis_index("section")
    first_docs = lax.dynamic_index_in_dim(forward_docs, section_index, 0, keepdims=False)
    back_docs = lax.dynamic_index_in_dim(backward_docs, section_index, 0, keepdims=False)
    gain_row = norm_gain[0]
    weights = (query_weight[0], key_matrix[0], value_matrix[0])
    forward_hidden = forward_rows[0].astype(jnp.float32)
    forward_normed = (forward_hidden * token_scale(forward_hidden) * gain_row).astype(jnp.bfloat16)
    back_hidden = saved_rows[0].astype(jnp.float32)
    back_scale = token_scale(back_hidden)
    back_normed = (back_hidden * back_scale * gain_row).astype(jnp.bfloat16)
    forward_whole = lax.all_gather(forward_normed, "seq", axis=0, tiled=True)
    query_rows_local, key_rows, value_rows, cosines, sines = heads_inputs(forward_whole, weights)
    mixed_rows = attend(query_rows_local, key_rows, value_rows, first_docs)
    mixed_rows = lax.all_to_all(mixed_rows, "seq", split_axis=0, concat_axis=1, tiled=True)
    first_out = (forward_hidden + mixed_rows.astype(jnp.float32)).astype(jnp.bfloat16)
    section_output = passed_along(first_out, "section", 1)
    back_whole = lax.all_gather(back_normed, "seq", axis=0, tiled=True)
    head_gradients = lax.all_to_all(output_grad[0], "seq", split_axis=1, concat_axis=0, tiled=True)
    query_rows_local, key_rows, value_rows, cosines, sines = heads_inputs(back_whole, weights)
    query_grad, key_grad, value_grad = attend_back(
        query_rows_local, key_rows, value_rows, head_gradients, back_docs, cosines, sines
    )
    term = jnp.einsum("tc,rc->tr", query_grad, weights[0], preferred_element_type=jnp.float32)
    term = term + jnp.einsum("tc,rc->tr", key_grad, weights[1], preferred_element_type=jnp.float32)
    input_sum = lax.psum_scatter(
        (
            term
            + jnp.einsum("tc,rc->tr", value_grad, weights[2], preferred_element_type=jnp.float32)
        ).astype(jnp.bfloat16),
        "seq",
        scatter_dimension=0,
        tiled=True,
    ).astype(jnp.float32)
    gained = gain_row * input_sum
    inner_sum = jnp.sum(back_hidden * gained, axis=-1, keepdims=True)
    norm_part = (
        back_scale * gained
        - back_hidden * (back_scale * back_scale * back_scale) * inner_sum / MODEL_WIDTH
    )
    first_grad = (output_grad[0].astype(jnp.float32) + norm_part).astype(jnp.bfloat16)
    input_grad = passed_along(first_grad, "section", -1)
    return (section_output[None], input_grad[None])


def solution(mesh):
    placed = (
        P("section", "seq", None),
        P("section", "seq", None),
        P("section", "seq", None),
        P(),
        P(),
        P("section", None),
        P("section", None, "seq"),
        P("section", None, "seq"),
        P("section", None, "seq"),
    )
    return jax.shard_map(
        body,
        mesh=mesh,
        in_specs=placed,
        out_specs=(P("section", "seq", None), P("section", "seq", None)),
        check_vma=False,
    )
```

profile of v0, /device:TPU:1, one launch (start us, length us, event | category | flops | bytes accessed | tf_op | source)
XLA Modules:
  0.0 678.1 jit_solution(13444456036712751143)
XLA Ops:
  7.2 1.7 fusion.29
  8.9 1.5 fusion.33
  11.5 3.5 fusion.35
  16.2 1.4 copy.43
  17.6 6.2 all-to-all-start.1
  24.3 6.4 copy.76
  34.4 1.7 fusion.48
  36.1 6.0 all-to-all-done.1
  42.1 1.1 fusion.146
  43.2 2.0 reshape.530
  45.2 2.0 reshape.532
  47.1 148.6 %all-gather.5.cloned.1.call-done = bf16[1024,4096]{1,0:T(8,128)(2,1)} async-done(((bf16[128,4096]{1,0:T(8,128)(2,1)}), bf16[1024,4096]{1,0:T(8,128)(2,1)}) %all-gather.5.cloned.1.call-update) | async-done | bytes 8388624 | tf_op jit(solution)/shard_map/all_gather | solution.py:195
  195.7 6.4 convolution_bitcast_fusion
  202.1 1.2 subtract_convert_fusion.5
  203.3 5.8 fusion.3
  209.2 163.2 %all-gather.3.cloned.1.call-done = bf16[1024,4096]{1,0:T(8,128)(2,1)} async-done(((bf16[128,4096]{1,0:T(8,128)(2,1)}), bf16[1024,4096]{1,0:T(8,128)(2,1)}) %all-gather.3.cloned.1.call-update) | async-done | bytes 8388624 | tf_op jit(solution)/shard_map/all_gather | solution.py:189
  372.4 8.5 %fusion.5 = f32[1024,4,128]{0,2,1:T(8,128)S(1)} fusion(bf16[4,128,4096]{2,1,0:T(8,128)(2,1)} %bitcast.349, bf16[1024,4096]{1,0:T(8,128)(2,1)} %all-gather.3.cloned.1.call-done), kind=kOutput, calls=%fused_computation.10 | convolution fusion | flops 4294967296 | bytes 14680064 | tf_op jit(solution)/shard_map/dot_general | solution.py:151
  380.9 1.7 subtract_convert_fusion
  384.6 1.4 fusion.81
  386.0 1.2 slice-done.5
  387.5 2.3 convolution_convert_fusion
  389.8 1.8 fusion.15
  391.6 1.4 fusion.42
  394.3 1.6 fusion.8
  395.9 2.3 fusion.11
  398.3 5.3 fusion
  403.5 2.6 fusion.78
  406.2 5.1 fusion.12
  412.1 1.5 fusion.74
  413.8 2.9 convolution_bitcast_fusion.1
  416.8 1.3 fusion.120
  418.9 8.6 %fusion.20 = f32[1024,4096]{1,0:T(8,128)} fusion(bf16[1024,512]{0,1:T(8,128)(2,1)S(1)} %pad_maximum_fusion.1, bf16[1,4096,512]{2,1,0:T(8,128)(2,1)S(1)} %copy-done.6), kind=kOutput, calls=%fused_computation.32 | convolution fusion | flops 4294967296 | bytes 22020096 | tf_op jit(solution)/shard_map/tc,rc->tr/dot_general | solution.py:201
  427.5 8.1 %fusion.86 = f32[1024,4096]{1,0:T(8,128)} fusion(bf16[1024,128]{0,1:T(8,128)(2,1)S(1)} %pad_maximum_fusion.7, bf16[1,4096,128]{2,1,0:T(8,128)(2,1)S(1)} %copy-done), kind=kOutput, calls=%fused_computation.105 | convolution fusion | flops 1073741824 | bytes 18087936 | tf_op jit(solution)/shard_map/tc,rc->tr/dot_general | solution.py:202
  435.6 15.3 %add_convert_fusion = bf16[1024,4096]{1,0:T(8,128)(2,1)} fusion(f32[1024,4096]{1,0:T(8,128)} %fusion.20, f32[1024,4096]{1,0:T(8,128)} %fusion.86, bf16[1024,128]{1,0:T(8,128)(2,1)S(1)} %fusion.78, bf16[1,4096,128]{2,1,0:T(8,128)(2,1)S(1)} %copy-done.11), kind=kOutput, calls=%fused_computation | convolution fusion | flops 1086324736 | bytes 43253760 | tf_op jit(solution)/shard_map/tc,rc->tr/dot_general | solution.py:206
  454.1 1.6 fusion.7
  455.9 2.3 convolution_convert_fusion.1
  458.3 2.3 fusion.9
  460.6 1.6 fusion.66
  462.1 2.9 fusion.60
  465.8 29.1 %all_to_all.29 = bf16[8,128,512]{2,1,0:T(8,128)(2,1)S(1)} all-to-all(bf16[8,128,512]{2,1,0:T(8,128)(2,1)S(1)} %bitcast.353), channel_id=1, replica_groups=mesh['section'=16,'seq'=8] {'seq'}, dimensions={0} | all-to-all | bytes 2097152 | tf_op jit(solution)/shard_map/all_to_all | solution.py:192
  496.1 1.2 fusion.32
  497.2 3.3 collective-permute-start
  500.5 147.7 %reduce-scatter.2.cloned.1.call-done = bf16[128,4096]{1,0:T(8,128)(2,1)} async-done(((bf16[1024,4096]{1,0:T(8,128)(2,1)}), bf16[128,4096]{1,0:T(8,128)(2,1)}) %reduce-scatter.2.cloned.1.call-update) | async-done | bytes 1048592 | tf_op jit(solution)/shard_map/reduce_scatter | solution.py:203
  648.2 1.6 fusion.41
  649.9 2.1 fusion.40
  652.0 2.5 collective-permute-start.1
  654.5 13.6 %collective-permute-done.1 = bf16[128,4096]{1,0:T(8,128)(2,1)S(1)} collective-permute-done((bf16[128,4096]{1,0:T(8,128)(2,1)S(1)}, bf16[128,4096]{1,0:T(8,128)(2,1)S(1)}, u32[]{:S(2)}, u32[]{:S(2)}) %collective-permute-start.1) | collective-permute-done | bytes 1048608 | tf_op jit(solution)/shard_map/ppermute | solution.py:15
  668.1 2.3 copy.93
  (95 shorter events, 18.0 us)
Async XLA Ops:
  7.2 188.5 %copy-start = (bf16[1,4096,128]{2,1,0:T(8,128)(2,1)S(1)}, bf16[1,4096,128]{2,1,0:T(8,128)(2,1)}, u32[]{:S(2)}) copy-start(bf16[1,4096,128]{2,1,0:T(8,128)(2,1)} %param.28) | copy-start | bytes 3145732
  7.2 8.6 %copy-start.4 = (bf16[1,128,4096]{2,1,0:T(8,128)(2,1)S(1)}, bf16[1,128,4096]{2,1,0:T(8,128)(2,1)}, u32[]{:S(2)}) copy-start(bf16[1,128,4096]{2,1,0:T(8,128)(2,1)} %param.23) | copy-start | bytes 3145732
  7.2 188.5 %all-gather.5.cloned.1.call-start = ((), (), s32[]{:S(2)}) async-start(), calls=%async_computation.4 | async-start | bytes 9437184 | tf_op jit(solution)/shard_map/all_gather | solution.py:195
  10.9 0.6 copy-start.20
  15.0 357.4 %all-gather.3.cloned.1.call-start = ((), (), s32[]{:S(2)}) async-start(), calls=%async_computation.3 | async-start | bytes 9437184 | tf_op jit(solution)/shard_map/all_gather | solution.py:189
  17.6 24.6 %all-to-all-start.1 = ((bf16[128,8,512]{2,0,1:T(8,128)(2,1)}), bf16[128,8,512]{2,0,1:T(8,128)(2,1)S(1)}, u32[]{:S(2)}, u32[]{:S(2)}) async-start(bf16[128,8,512]{2,0,1:T(8,128)(2,1)} %copy.43), calls=%async_computation.1 | async-start | bytes 2097152 | tf_op jit(solution)/shard_map/all_to_all | solution.py:196
  23.8 624.4 %reduce-scatter.2.cloned.1.call-start = ((), (), s32[]{:S(2)}) async-start(), calls=%async_computation.5 | async-start | bytes 9437184 | tf_op jit(solution)/shard_map/reduce_scatter | solution.py:203
  195.7 7.6 %copy-start.1 = (bf16[1024,4096]{1,0:T(8,128)(2,1)S(1)}, bf16[1024,4096]{1,0:T(8,128)(2,1)}, u32[]{:S(2)}) copy-start(bf16[1024,4096]{1,0:T(8,128)(2,1)} %all-gather.5.cloned.1.call-done) | copy-start | bytes 25165828
  195.7 7.6 %copy-start.7 = (bf16[512,4096]{1,0:T(8,128)(2,1)S(1)}, bf16[512,4096]{1,0:T(8,128)(2,1)}, u32[]{:S(2)}) copy-start(bf16[512,4096]{1,0:T(8,128)(2,1)} %copy.76) | copy-start | bytes 12582916
  372.4 8.5 %copy-start.9 = (f32[1024,4,128]{0,2,1:T(8,128)S(1)}, f32[1024,4,128]{0,2,1:T(8,128)}, u32[]{:S(2)}) copy-start(f32[1024,4,128]{0,2,1:T(8,128)} %fusion.3) | copy-start | bytes 6291460
  382.6 2.0 copy-start.16
  383.5 2.5 slice-start.4
  384.6 2.6 slice-start.5
  384.6 2.8 copy-start.10
  395.9 2.3 copy-start.15
  398.3 15.5 %slice-start = ((s8[8388608]{0:T(1024)(128)(4,1)}), s8[4194304]{0:T(1024)(128)(4,1)S(1)}, s32[]{:S(2)}) async-start(s8[8388608]{0:T(1024)(128)(4,1)} %bitcast.340), calls=%async_computation.6 | async-start | bytes 8388608
  403.5 10.3 %slice-start.1 = ((s8[8388608]{0:T(1024)(128)(4,1)}), s8[4194304]{0:T(1024)(128)(4,1)S(1)}, s32[]{:S(2)}) async-start(s8[8388608]{0:T(1024)(128)(4,1)} %bitcast.340), calls=%async_computation.7 | async-start | bytes 8388608
  412.1 1.5 copy-start.13
  412.1 1.5 copy-start.14
  413.8 4.2 copy-start.12
  416.7 2.2 copy-start.6
  427.5 8.1 %copy-start.11 = (bf16[1,4096,128]{2,1,0:T(8,128)(2,1)S(1)}, bf16[1,4096,128]{2,1,0:T(8,128)(2,1)}, u32[]{:S(2)}) copy-start(bf16[1,4096,128]{2,1,0:T(8,128)(2,1)} %param.29) | copy-start | bytes 3145732
  450.9 1.0 copy-start.17
  450.9 1.2 copy-start.18
  452.1 2.0 copy-start.8
  452.1 3.6 slice-start.2
  453.0 2.9 slice-start.3
  494.8 1.2 copy-start.3
  495.1 153.1 %copy-start.2 = (bf16[1,128,4096]{2,1,0:T(8,128)(2,1)S(1)}, bf16[1,128,4096]{2,1,0:T(8,128)(2,1)}, u32[]{:S(2)}) copy-start(bf16[1,128,4096]{2,1,0:T(8,128)(2,1)} %param.22) | copy-start | bytes 3145732
  495.1 153.0 %copy-start.19 = (f32[1,4096]{1,0:T(1,128)S(1)}, f32[1,4096]{1,0:T(1,128)}, u32[]{:S(2)}) copy-start(f32[1,4096]{1,0:T(1,128)} %param.26) | copy-start | bytes 49156
  495.4 154.4 %copy-start.5 = (bf16[1,128,4096]{2,1,0:T(8,128)(2,1)S(1)}, bf16[1,128,4096]{2,1,0:T(8,128)(2,1)}, u32[]{:S(2)}) copy-start(bf16[1,128,4096]{2,1,0:T(8,128)(2,1)} %param.23) | copy-start | bytes 3145732
  495.4 154.4 %copy-start.21 = (f32[128]{0:T(128)S(1)}, f32[128]{0:T(128)}, u32[]{:S(2)}) copy-start(f32[128]{0:T(128)} %copy-done.20) | copy-start | bytes 1540
  495.4 154.4 %copy-start.22 = (f32[128]{0:T(128)S(1)}, f32[128]{0:T(128)}, u32[]{:S(2)}) copy-start(f32[128]{0:T(128)} %get-tuple-element.102) | copy-start | bytes 1540
  497.2 157.2 %collective-permute-start = (bf16[128,4096]{1,0:T(8,128)(2,1)}, bf16[128,4096]{1,0:T(8,128)(2,1)}, u32[]{:S(2)}, u32[]{:S(2)}) collective-permute-start(bf16[128,4096]{1,0:T(8,128)(2,1)} %fusion.32), channel_id=1, source_target_pairs={{0,8},{8,16},{16,24},{24,32},{32,40},{40,48},{48,56},{56,64},{64,7... | collective-permute-start | bytes 3145736 | tf_op jit(solution)/shard_map/ppermute | solution.py:15
  652.0 16.1 %collective-permute-start.1 = (bf16[128,4096]{1,0:T(8,128)(2,1)S(1)}, bf16[128,4096]{1,0:T(8,128)(2,1)S(1)}, u32[]{:S(2)}, u32[]{:S(2)}) collective-permute-start(bf16[128,4096]{1,0:T(8,128)(2,1)S(1)} %fusion.40), channel_id=1, source_target_pairs={{8,0},{16,8},{24,16},{32,24},{40,32},{48,40},{56,48},{64,56},{72,6... | collective-permute-start | bytes 3145736 | tf_op jit(solution)/shard_map/ppermute | solution.py:15
Sparse Core Ops, SparseCore 0:
  15.2 180.4 all-gather.4
  197.9 174.4 all-gather.2
  451.0 197.0 reduce-scatter.1
where the time goes:
time: 681 us; the launch traced here: 678 us
  waiting for transfers between devices  480 us (70%)
  matrix products  84.5 us (12%)
  other arithmetic  34.4 us (5%)
  blocking collectives  29.1 us (4%)
  local copies, waits for them, and re-layouts  23.2 us (3%)
  between operations  14.5 us (2%)
  starting transfers between devices  12.6 us (2%)
    all_gather x1, waiting for transfers between devices, body(): forward_whole = lax.all_gather(forward_normed, 'seq', axis=0, tiled=True)  163 us
    all_gather x1, waiting for transfers between devices, body(): back_whole = lax.all_gather(back_normed, 'seq', axis=0, tiled=True)  149 us
    reduce_scatter x1, waiting for transfers between devices, body(): lax.psum_scatter((term + jnp.einsum('tc,rc->tr', value_grad, weights[2],...  148 us
    all_to_all x1, blocking collectives, body(): lax.all_to_all(mixed_rows, 'seq', split_axis=0, concat_axis=1, tiled=True)  29.1 us
    dot_general x1, matrix products, body(): jnp.einsum('tc,rc->tr', value_grad, weights[2], preferred_element_type=jn...  15.3 us
    dot_general x2, matrix products, heads_inputs(): jnp.dot(rows_whole, query_weight, preferred_element_type=jnp.float32)  14.3 us
  transfers between devices with their start and end apart: 6, of which 5 were waited for; matrix products, arithmetic and copies ran while one was open for 8% of the time, Pallas kernels for 0%

commit v1 on v0

--- a/solution.py
+++ b/solution.py
@@ -186,7 +186,9 @@
     back_hidden = saved_rows[0].astype(jnp.float32)
     back_scale = token_scale(back_hidden)
     back_normed = (back_hidden * back_scale * gain_row).astype(jnp.bfloat16)
-    forward_whole = lax.all_gather(forward_normed, "seq", axis=0, tiled=True)
+    forward_whole = jnp.concatenate(
+        lax.all_to_all(jnp.stack([forward_normed] * lax.axis_size("seq")), "seq", 0, 0), axis=0
+    )
     query_rows_local, key_rows, value_rows, cosines, sines = heads_inputs(forward_whole, weights)
     mixed_rows = attend(query_rows_local, key_rows, value_rows, first_docs)
     mixed_rows = lax.all_to_all(mixed_rows, "seq", split_axis=0, concat_axis=1, tiled=True)

time: 681 us -> 585 us (0.86)
  waiting for transfers between devices: 480 us -> 365 us
  starting transfers between devices: 12.6 us -> 26.6 us
    all_gather x1 -> x0, waiting for transfers between devices: 163 us -> none  [body(): forward_whole = lax.all_gather(forward_normed, 'seq', axis=0, tiled=True)]
    all_to_all x0 -> x1, waiting for transfers between devices: none -> 122 us  [body(): lax.all_to_all(jnp.stack([forward_normed] * lax.axis_size('seq')), 'seq',...]
    all_gather x1, waiting for transfers between devices: 149 us -> 73 us  [body(): back_whole = lax.all_gather(back_normed, 'seq', axis=0, tiled=True)]
    all_to_all x0 -> x1, starting transfers between devices: none -> 13.2 us  [body(): lax.all_to_all(jnp.stack([forward_normed] * lax.axis_size('seq')), 'seq',...]
    all_to_all x1, waiting for transfers between devices: 6.01 us -> 14 us  [body(): lax.all_to_all(output_grad[0], 'seq', split_axis=1, concat_axis=0, tiled=...]
  transfers between devices with their start and end apart: 6 -> 6, of which waited for: 5 -> 5; matrix products, arithmetic and copies ran while one was open for 8% -> 12% of each run, Pallas kernels for 0% -> 0%
where the time goes in v1:
time: 585 us; the launch traced here: 581 us
  waiting for transfers between devices  365 us (62%)
  matrix products  88.7 us (15%)
  other arithmetic  33.7 us (6%)
  local copies, waits for them, and re-layouts  28.9 us (5%)
  starting transfers between devices  26.6 us (5%)
  blocking collectives  23.8 us (4%)
  between operations  14.9 us (3%)
    reduce_scatter x1, waiting for transfers between devices, body(): lax.psum_scatter((term + jnp.einsum('tc,rc->tr', value_grad, weights[2],...  144 us
    all_to_all x1, waiting for transfers between devices, body(): lax.all_to_all(jnp.stack([forward_normed] * lax.axis_size('seq')), 'seq',...  122 us
    all_gather x1, waiting for transfers between devices, body(): back_whole = lax.all_gather(back_normed, 'seq', axis=0, tiled=True)  73 us
    all_to_all x1, blocking collectives, body(): lax.all_to_all(mixed_rows, 'seq', split_axis=0, concat_axis=1, tiled=True)  23.8 us
    dot_general x1, matrix products, body(): jnp.einsum('tc,rc->tr', value_grad, weights[2], preferred_element_type=jn...  15.4 us
    all_to_all x1, waiting for transfers between devices, body(): lax.all_to_all(output_grad[0], 'seq', split_axis=1, concat_axis=0, tiled=...  14 us
    all_to_all x1, starting transfers between devices, body(): lax.all_to_all(jnp.stack([forward_normed] * lax.axis_size('seq')), 'seq',...  13.2 us
    dot_general x2, matrix products, heads_inputs(): jnp.dot(rows_whole, key_matrix, preferred_element_type=jnp.float32)  12.9 us
  transfers between devices with their start and end apart: 6, of which 5 were waited for; matrix products, arithmetic and copies ran while one was open for 12% of the time, Pallas kernels for 0%

profile of v1, /device:TPU:1, one launch (start us, length us, event | category | flops | bytes accessed | tf_op | source)
XLA Modules:
  0.0 581.3 jit_solution(6623867737745150664)
XLA Ops:
  7.2 1.7 fusion.33
  10.0 2.5 fusion.35
  14.3 6.2 %all-to-all-start.2 = ((bf16[128,8,512]{2,0,1:T(8,128)(2,1)}), bf16[128,8,512]{2,0,1:T(8,128)(2,1)}, u32[]{:S(2)}, u32[]{:S(2)}) async-start(bf16[128,8,512]{2,0,1:T(8,128)(2,1)} %copy.94), calls=%async_computation.2 | async-start | bytes 2097152 | tf_op jit(solution)/shard_map/all_to_all | solution.py:198
  21.7 1.5 fusion.86
  23.3 1.5 copy.79
  24.8 14.0 %all-to-all-done.2 = bf16[128,8,512]{2,0,1:T(8,128)(2,1)} async-done(((bf16[128,8,512]{2,0,1:T(8,128)(2,1)}), bf16[128,8,512]{2,0,1:T(8,128)(2,1)}, u32[]{:S(2)}, u32[]{:S(2)}) %all-to-all-start.2) | async-done | bytes 1048608 | tf_op jit(solution)/shard_map/all_to_all | solution.py:198
  38.7 4.4 stack.5
  43.1 13.2 %all-to-all-start = ((bf16[8,128,4096]{2,1,0:T(8,128)(2,1)}), bf16[8,128,4096]{2,1,0:T(8,128)(2,1)}, u32[]{:S(2)}, u32[]{:S(2)}) async-start(bf16[8,128,4096]{2,1,0:T(8,128)(2,1)} %stack.5), calls=%async_computation | async-start | bytes 16777216 | tf_op jit(solution)/shard_map/all_to_all | solution.py:190
  56.5 6.5 %copy.128 = bf16[512,4096]{1,0:T(8,128)(2,1)} copy(bf16[512,4096]{0,1:T(8,128)(2,1)} %bitcast.349) | data formatting | bytes 8388608 | tf_op jit(solution)/shard_map/dot_general | solution.py:151
  67.7 2.1 fusion.147
  69.8 2.0 reshape.548
  72.7 121.9 %all-to-all-done = bf16[8,128,4096]{2,1,0:T(8,128)(2,1)} async-done(((bf16[8,128,4096]{2,1,0:T(8,128)(2,1)}), bf16[8,128,4096]{2,1,0:T(8,128)(2,1)}, u32[]{:S(2)}, u32[]{:S(2)}) %all-to-all-start) | async-done | bytes 8388640 | tf_op jit(solution)/shard_map/all_to_all | solution.py:190
  194.6 6.4 %convolution_bitcast_fusion.1 = f32[1024,1,128]{0,2,1:T(8,128)S(1)} fusion(bf16[1024,4096]{1,0:T(8,128)(2,1)} %bitcast.3, bf16[1,4096,128]{2,1,0:T(8,128)(2,1)S(1)} %copy-done), kind=kOutput, calls=%fused_computation.83 | convolution fusion | flops 1073741824 | bytes 9961472 | tf_op jit(solution)/shard_map/dot_general | solution.py:152
  201.0 8.3 %fusion.149 = f32[1024,4,128]{0,2,1:T(8,128)} fusion(bf16[1024,4096,1]{1,0,2:T(8,128)(2,1)} %bitcast.11, bf16[4,128,4096]{2,1,0:T(8,128)(2,1)S(1)} %bitcast.350), kind=kOutput, calls=%fused_computation.199 | convolution fusion | flops 4294967296 | bytes 14680064 | tf_op jit(solution)/shard_map/dot_general | solution.py:151
  209.4 73.0 %all-gather.2.cloned.1.call-done = bf16[1024,4096]{1,0:T(8,128)(2,1)} async-done(((bf16[128,4096]{1,0:T(8,128)(2,1)}), bf16[1024,4096]{1,0:T(8,128)(2,1)}) %all-gather.2.cloned.1.call-update) | async-done | bytes 8388624 | tf_op jit(solution)/shard_map/all_gather | solution.py:197
  282.3 6.4 %convolution_bitcast_fusion = f32[1024,1,128]{0,2,1:T(8,128)S(1)} fusion(bf16[1024,4096]{1,0:T(8,128)(2,1)} %all-gather.2.cloned.1.call-done, bf16[1,4096,128]{2,1,0:T(8,128)(2,1)S(1)} %copy-done), kind=kOutput, calls=%fused_computation.82 | convolution fusion | flops 1073741824 | bytes 9961472 | tf_op jit(solution)/shard_map/dot_general | solution.py:152
  288.8 1.4 subtract_convert_fusion.5
  290.2 4.5 fusion.3
  294.7 1.7 subtract_convert_fusion
  298.4 2.1 fusion.81
  300.5 2.3 convolution_convert_fusion
  302.8 1.7 fusion.13
  304.6 1.9 fusion.42
  307.7 1.7 fusion.6
  309.4 2.1 fusion.9
  311.6 3.5 fusion
  315.1 2.7 fusion.78
  317.8 2.9 fusion.10
  321.5 1.5 fusion.74
  323.3 2.1 fusion.121
  325.8 8.2 %fusion.18 = f32[1024,4096]{1,0:T(8,128)} fusion(bf16[1024,512]{0,1:T(8,128)(2,1)S(1)} %pad_maximum_fusion.1, bf16[1,4096,512]{2,1,0:T(8,128)(2,1)S(1)} %copy-done.6), kind=kOutput, calls=%fused_computation.30 | convolution fusion | flops 4294967296 | bytes 22020096 | tf_op jit(solution)/shard_map/tc,rc->tr/dot_general | solution.py:203
  334.0 8.1 %fusion.87 = f32[1024,4096]{1,0:T(8,128)} fusion(bf16[1024,128]{0,1:T(8,128)(2,1)S(1)} %pad_maximum_fusion.7, bf16[1,4096,128]{2,1,0:T(8,128)(2,1)S(1)} %copy-done), kind=kOutput, calls=%fused_computation.104 | convolution fusion | flops 1073741824 | bytes 18087936 | tf_op jit(solution)/shard_map/tc,rc->tr/dot_general | solution.py:204
  342.1 15.4 %add_convert_fusion = bf16[1024,4096]{1,0:T(8,128)(2,1)} fusion(f32[1024,4096]{1,0:T(8,128)} %fusion.18, f32[1024,4096]{1,0:T(8,128)} %fusion.87, bf16[1024,128]{1,0:T(8,128)(2,1)S(1)} %fusion.78, bf16[1,4096,128]{2,1,0:T(8,128)(2,1)S(1)} %copy-done.12), kind=kOutput, calls=%fused_computation | convolution fusion | flops 1086324736 | bytes 43253760 | tf_op jit(solution)/shard_map/tc,rc->tr/dot_general | solution.py:208
  357.7 5.8 convolution_convert_fusion.1
  365.6 1.7 fusion.5
  367.2 2.3 fusion.7
  369.6 1.5 fusion.66
  371.1 2.9 fusion.60
  375.5 23.8 %all_to_all.34 = bf16[8,128,512]{2,1,0:T(8,128)(2,1)} all-to-all(bf16[8,128,512]{2,1,0:T(8,128)(2,1)} %bitcast.353), channel_id=1, replica_groups=mesh['section'=16,'seq'=8] {'seq'}, dimensions={0} | all-to-all | bytes 2097152 | tf_op jit(solution)/shard_map/all_to_all | solution.py:194
  399.4 2.3 copy.90
  401.6 2.5 fusion.30
  404.1 4.5 collective-permute-start
  408.6 144.5 %reduce-scatter.2.cloned.1.call-done = bf16[128,4096]{1,0:T(8,128)(2,1)} async-done(((bf16[1024,4096]{1,0:T(8,128)(2,1)}), bf16[128,4096]{1,0:T(8,128)(2,1)}) %reduce-scatter.2.cloned.1.call-update) | async-done | bytes 1048592 | tf_op jit(solution)/shard_map/reduce_scatter | solution.py:205
  553.1 1.6 fusion.41
  554.7 2.4 fusion.40
  557.2 2.5 collective-permute-start.1
  559.7 2.3 copy.105
  562.0 11.3 %collective-permute-done.1 = bf16[128,4096]{1,0:T(8,128)(2,1)S(1)} collective-permute-done((bf16[128,4096]{1,0:T(8,128)(2,1)S(1)}, bf16[128,4096]{1,0:T(8,128)(2,1)S(1)}, u32[]{:S(2)}, u32[]{:S(2)}) %collective-permute-start.1) | collective-permute-done | bytes 1048608 | tf_op jit(solution)/shard_map/ppermute | solution.py:15
  (97 shorter events, 19.3 us)
Async XLA Ops:
  7.2 187.4 %copy-start = (bf16[1,4096,128]{2,1,0:T(8,128)(2,1)S(1)}, bf16[1,4096,128]{2,1,0:T(8,128)(2,1)}, u32[]{:S(2)}) copy-start(bf16[1,4096,128]{2,1,0:T(8,128)(2,1)} %param.28) | copy-start | bytes 3145732
  7.2 5.3 copy-start.5
  7.2 275.1 %all-gather.2.cloned.1.call-start = ((), (), s32[]{:S(2)}) async-start(), calls=%async_computation.4 | async-start | bytes 9437184 | tf_op jit(solution)/shard_map/all_gather | solution.py:197
  9.4 0.5 copy-start.24
  12.5 8.0 %copy-start.10 = (bf16[1,128,4096]{2,1,0:T(8,128)(2,1)S(1)}, bf16[1,128,4096]{2,1,0:T(8,128)(2,1)}, u32[]{:S(2)}) copy-start(bf16[1,128,4096]{2,1,0:T(8,128)(2,1)} %param.21) | copy-start | bytes 3145732
  12.9 8.8 %copy-start.20 = (f32[1,4096]{1,0:T(1,128)S(1)}, f32[1,4096]{1,0:T(1,128)}, u32[]{:S(2)}) copy-start(f32[1,4096]{1,0:T(1,128)} %param.26) | copy-start | bytes 49156
  14.3 24.4 %all-to-all-start.2 = ((bf16[128,8,512]{2,0,1:T(8,128)(2,1)}), bf16[128,8,512]{2,0,1:T(8,128)(2,1)}, u32[]{:S(2)}, u32[]{:S(2)}) async-start(bf16[128,8,512]{2,0,1:T(8,128)(2,1)} %copy.94), calls=%async_computation.2 | async-start | bytes 2097152 | tf_op jit(solution)/shard_map/all_to_all | solution.py:198
  21.2 21.9 %copy-start.3 = (bf16[1,128,4096]{1,2,0:T(8,128)(2,1)}, bf16[1,128,4096]{1,2,0:T(8,128)(2,1)S(1)}, u32[]{:S(2)}) copy-start(bf16[1,128,4096]{1,2,0:T(8,128)(2,1)S(1)} %copy.78) | copy-start | bytes 3145732
  43.1 151.5 %all-to-all-start = ((bf16[8,128,4096]{2,1,0:T(8,128)(2,1)}), bf16[8,128,4096]{2,1,0:T(8,128)(2,1)}, u32[]{:S(2)}, u32[]{:S(2)}) async-start(bf16[8,128,4096]{2,1,0:T(8,128)(2,1)} %stack.5), calls=%async_computation | async-start | bytes 16777216 | tf_op jit(solution)/shard_map/all_to_all | solution.py:190
  56.3 496.8 %reduce-scatter.2.cloned.1.call-start = ((), (), s32[]{:S(2)}) async-start(), calls=%async_computation.5 | async-start | bytes 9437184 | tf_op jit(solution)/shard_map/reduce_scatter | solution.py:205
  194.6 6.4 %copy-start.7 = (bf16[512,4096]{1,0:T(8,128)(2,1)S(1)}, bf16[512,4096]{1,0:T(8,128)(2,1)}, u32[]{:S(2)}) copy-start(bf16[512,4096]{1,0:T(8,128)(2,1)} %copy.128) | copy-start | bytes 12582916
  282.3 7.8 %copy-start.1 = (bf16[1024,4096]{1,0:T(8,128)(2,1)S(1)}, bf16[1024,4096]{1,0:T(8,128)(2,1)}, u32[]{:S(2)}) copy-start(bf16[1024,4096]{1,0:T(8,128)(2,1)} %all-gather.2.cloned.1.call-done) | copy-start | bytes 25165828
  282.3 7.8 %copy-start.8 = (bf16[512,4096]{1,0:T(8,128)(2,1)S(1)}, bf16[512,4096]{1,0:T(8,128)(2,1)}, u32[]{:S(2)}) copy-start(bf16[512,4096]{1,0:T(8,128)(2,1)} %copy.128) | copy-start | bytes 12582916
  290.2 4.5 copy-start.9
  296.4 2.0 copy-start.17
  298.4 2.1 copy-start.11
  302.8 1.8 copy-start.27
  309.4 2.1 copy-start.16
  309.4 2.1 copy-start.28
  311.6 3.5 copy-start.29
  321.5 1.5 copy-start.14
  321.5 1.5 copy-start.15
  321.5 3.9 copy-start.13
  323.2 2.6 copy-start.6
  334.0 8.1 %copy-start.12 = (bf16[1,4096,128]{2,1,0:T(8,128)(2,1)S(1)}, bf16[1,4096,128]{2,1,0:T(8,128)(2,1)}, u32[]{:S(2)}) copy-start(bf16[1,4096,128]{2,1,0:T(8,128)(2,1)} %param.29) | copy-start | bytes 3145732
  357.7 5.9 %copy-start.18 = (bf16[1024,4,64]{0,2,1:T(8,128)(2,1)S(1)}, bf16[1024,4,64]{0,2,1:T(8,128)(2,1)}, u32[]{:S(2)}) copy-start(bf16[1024,4,64]{0,2,1:T(8,128)(2,1)} %get-tuple-element.90) | copy-start | bytes 1572868
  357.7 5.8 %copy-start.19 = (bf16[1024,4,64]{0,2,1:T(8,128)(2,1)S(1)}, bf16[1024,4,64]{0,2,1:T(8,128)(2,1)}, u32[]{:S(2)}) copy-start(bf16[1024,4,64]{0,2,1:T(8,128)(2,1)} %get-tuple-element.91) | copy-start | bytes 1572868
  357.7 5.8 %copy-start.22 = (bf16[1024,1,64]{0,2,1:T(8,128)(2,1)S(1)}, bf16[1024,1,64]{0,2,1:T(8,128)(2,1)}, u32[]{:S(2)}) copy-start(bf16[1024,1,64]{0,2,1:T(8,128)(2,1)} %get-tuple-element.104) | copy-start | bytes 393220
  357.7 5.8 %copy-start.23 = (bf16[1024,1,64]{0,2,1:T(8,128)(2,1)S(1)}, bf16[1024,1,64]{0,2,1:T(8,128)(2,1)}, u32[]{:S(2)}) copy-start(bf16[1024,1,64]{0,2,1:T(8,128)(2,1)} %get-tuple-element.105) | copy-start | bytes 393220
  374.0 27.6 %copy-start.4 = (bf16[1,128,4096]{1,2,0:T(8,128)(2,1)S(1)}, bf16[1,128,4096]{1,2,0:T(8,128)(2,1)}, u32[]{:S(2)}) copy-start(bf16[1,128,4096]{1,2,0:T(8,128)(2,1)} %copy-done.3) | copy-start | bytes 3145732
  375.5 177.5 %copy-start.2 = (bf16[1,128,4096]{2,1,0:T(8,128)(2,1)S(1)}, bf16[1,128,4096]{2,1,0:T(8,128)(2,1)}, u32[]{:S(2)}) copy-start(bf16[1,128,4096]{2,1,0:T(8,128)(2,1)} %param.22) | copy-start | bytes 3145732
  375.5 177.5 %copy-start.21 = (f32[1,4096]{1,0:T(1,128)S(1)}, f32[1,4096]{1,0:T(1,128)}, u32[]{:S(2)}) copy-start(f32[1,4096]{1,0:T(1,128)} %param.26) | copy-start | bytes 49156
  399.4 155.3 %copy-start.25 = (f32[128]{0:T(128)S(1)}, f32[128]{0:T(128)}, u32[]{:S(2)}) copy-start(f32[128]{0:T(128)} %copy-done.24) | copy-start | bytes 1540
  399.4 155.4 %copy-start.26 = (f32[128]{0:T(128)S(1)}, f32[128]{0:T(128)}, u32[]{:S(2)}) copy-start(f32[128]{0:T(128)} %get-tuple-element.102) | copy-start | bytes 1540
  404.1 155.6 %collective-permute-start = (bf16[128,4096]{0,1:T(8,128)(2,1)}, bf16[128,4096]{0,1:T(8,128)(2,1)}, u32[]{:S(2)}, u32[]{:S(2)}) collective-permute-start(bf16[128,4096]{0,1:T(8,128)(2,1)} %fusion.30), channel_id=1, source_target_pairs={{0,8},{8,16},{16,24},{24,32},{32,40},{40,48},{48,56},{56,64},{64,7... | collective-permute-start | bytes 3145736 | tf_op jit(solution)/shard_map/ppermute | solution.py:15
  557.2 16.1 %collective-permute-start.1 = (bf16[128,4096]{1,0:T(8,128)(2,1)S(1)}, bf16[128,4096]{1,0:T(8,128)(2,1)S(1)}, u32[]{:S(2)}, u32[]{:S(2)}) collective-permute-start(bf16[128,4096]{1,0:T(8,128)(2,1)S(1)} %fusion.40), channel_id=1, source_target_pairs={{8,0},{16,8},{24,16},{32,24},{40,32},{48,40},{56,48},{64,56},{72,6... | collective-permute-start | bytes 3145736 | tf_op jit(solution)/shard_map/ppermute | solution.py:15
Sparse Core Ops, SparseCore 0:
  12.6 269.6 all-gather.1
  357.6 195.4 reduce-scatter.1
